TPU v7x, 256 devices: a whole 4x4x8 slice. The times are simulated.
256 devices in a mesh: node: 16 (over z, core), head: 16 (over x, y).
Axes of the slice: x: 4, y: 4, z: 8, core: 2. Of those that a mesh axis runs over, the one named last changes fastest.
Arguments:
- features: bfloat16 [65536, 1024], P(('node', 'head')), may hold values from -6 to 6
- attn_gain: float32 [1024], replicated, may hold values from 0.25 to 1.75
- qkv_weight: bfloat16 [1024, 16, 192], P(None, 'head')
- out_weight: bfloat16 [1024, 1024], replicated, may hold values from -0.1875 to 0.1875
- feedforward_norm_gain: float32 [1024], replicated, may hold values from 0.25 to 1.75
- up_weight: bfloat16 [1024, 2048], replicated, may hold values from -0.1875 to 0.1875
- down_weight: bfloat16 [2048, 1024], replicated, may hold values from -0.125 to 0.125
- tile_pattern: int32 [512, 8], P('node'), may hold values from 0 to 511, as said below
- node_order: int32 [16, 4096], P('node'), may hold values from 0 to 4095, each once within a row
Outputs:
- updated: bfloat16 [65536, 1024], P(('node', 'head'))
Inputs may be any that keep to these rules, and one draw needn't show every extreme that they name: `tile_pattern`: row t names 8 different tiles; the first is t itself; all lie in partitions (tiles p * 32 to (p + 1) * 32 - 1) at cyclic distance at most 2 from t's partition; the second lies 2 partitions below t's and the third 2 above. `node_order`: each row lists every local row of its partition once.
All inputs are finite; a program needn't handle non-finite values.
Results may differ from a plain program's by a relative error of at most 0.0045.
Values may be sent and summed in bfloat16 or wider, within the bound.
A program may use at most 64 MiB of HBM per device.

v0:
```python
import math
import jax
import jax.numpy as jnp
from jax import lax
from jax.sharding import PartitionSpec as P

D = 1024
HD = 64
TILE = 128
NNZ = 8
REACH = 2


def passed_along(x, axis, by):
    size = lax.axis_size(axis)
    return lax.ppermute(x, axis, [(i, (i + by) % size) for i in range(size)])


def layer_norm(values, gain):
    row_mean = jnp.mean(values, -1, keepdims=True)
    centred = values - row_mean
    variance = jnp.mean(centred * centred, -1, keepdims=True)
    return centred * lax.rsqrt(variance + 1e-05) * gain


def shards(
    features,
    attn_gain,
    qkv_weight,
    out_weight,
    feedforward_norm_gain,
    up_weight,
    down_weight,
    tile_pattern,
    node_order,
):
    own_rows = features.shape[0]
    local_heads = qkv_weight.shape[1]
    head_placements = lax.axis_size("head")
    partitions = lax.axis_size("node")
    rows_part = own_rows * head_placements
    query_tiles = rows_part // TILE
    normed = layer_norm(features.astype(jnp.float32), attn_gain).astype(jnp.bfloat16)
    reordered_weight = jnp.concatenate([qkv_weight[:, :, HD:], qkv_weight[:, :, :HD]], -1)
    local_weight = reordered_weight.reshape(D, local_heads * 3 * HD)
    projected = jnp.dot(
        lax.all_gather(normed, "head", axis=0, tiled=True),
        local_weight,
        preferred_element_type=jnp.float32,
    ).astype(jnp.bfloat16)
    projected = projected.reshape(rows_part, local_heads, 3 * HD)
    partition_permutation = node_order[0]
    keyval_rows = projected[:, :, : 2 * HD].reshape(rows_part, local_heads * 2 * HD)
    query_rows = projected[:, :, 2 * HD :].reshape(rows_part, local_heads * HD)
    keyval = jnp.take(keyval_rows, partition_permutation, axis=0)
    queries = jnp.take(query_rows, partition_permutation, axis=0)
    current = passed_along(keyval, "node", -REACH)
    blocks = [current]
    for cycle_step in range(2 * REACH):
        current = passed_along(current, "node", 1)
        blocks.append(current)
    window = jnp.stack(blocks[::-1])
    window_tiles = window.reshape((2 * REACH + 1) * query_tiles, TILE, local_heads * 2 * HD)
    partition = lax.axis_index("node")
    window_position = (
        tile_pattern // query_tiles - partition + REACH + partitions
    ) % partitions * query_tiles + tile_pattern % query_tiles
    tile_group = math.gcd(query_tiles, max(1, 512 // TILE))
    score_scale = 1.0 / math.sqrt(HD)

    def attend(item_pair):
        group_queries, columns = item_pair
        picked = jnp.take(window_tiles, columns.reshape(tile_group * NNZ), axis=0)
        picked = picked.reshape(tile_group, NNZ * TILE, local_heads, 2 * HD)
        key_rows = picked[..., :HD]
        value_rows = picked[..., HD:]
        query_block = group_queries.reshape(tile_group, TILE, local_heads, HD)
        scores = (
            jnp.einsum("gqhd,gmhd->ghqm", query_block, key_rows, preferred_element_type=jnp.float32)
            * score_scale
        )
        row_max = jnp.max(scores, -1, keepdims=True)
        expd = jnp.exp(scores - row_max)
        weight_arrays = (expd / jnp.sum(expd, -1, keepdims=True)).astype(jnp.bfloat16)
        result = jnp.einsum(
            "ghqm,gmhd->gqhd", weight_arrays, value_rows, preferred_element_type=jnp.float32
        ).astype(jnp.bfloat16)
        return result.reshape(tile_group * TILE, local_heads * HD)

    grouped_queries = queries.reshape(
        query_tiles // tile_group, tile_group * TILE, local_heads * HD
    )
    grouped_slots = window_position.reshape(query_tiles // tile_group, tile_group, NNZ)
    attended = lax.map(attend, (grouped_queries, grouped_slots)).reshape(
        rows_part, local_heads * HD
    )
    inverse_order = (
        jnp.zeros((rows_part,), jnp.int32)
        .at[partition_permutation]
        .set(jnp.arange(rows_part, dtype=jnp.int32))
    )
    restored = jnp.take(attended, inverse_order, axis=0)
    gathered_heads = lax.all_to_all(restored, "head", split_axis=0, concat_axis=1, tiled=True)
    residual = features.astype(jnp.float32) + jnp.dot(
        gathered_heads, out_weight, preferred_element_type=jnp.float32
    )
    mlp_input = layer_norm(residual, feedforward_norm_gain).astype(jnp.bfloat16)
    hidden = jax.nn.gelu(jnp.dot(mlp_input, up_weight, preferred_element_type=jnp.float32)).astype(
        jnp.bfloat16
    )
    return (residual + jnp.dot(hidden, down_weight, preferred_element_type=jnp.float32)).astype(
        jnp.bfloat16
    )


def solution(mesh):
    return jax.shard_map(
        shards,
        mesh=mesh,
        in_specs=(
            P(("node", "head"), None),
            P(),
            P(None, "head", None),
            P(),
            P(),
            P(),
            P(),
            P("node", None),
            P("node", None),
        ),
        out_specs=P(("node", "head"), None),
        check_vma=False,
    )
```

profile of v0, /device:TPU:96, one launch (start us, length us, event | category | flops | bytes accessed | tf_op | source)
XLA Modules:
  0.0 371.6 jit_solution(18285803736506806688)
XLA Ops:
  9.3 2.1 fusion.37
  11.5 77.8 %all-gather.2.cloned.1.call-done = bf16[4096,1024]{1,0:T(8,128)(2,1)} async-done(((bf16[256,1024]{1,0:T(8,128)(2,1)}), bf16[4096,1024]{1,0:T(8,128)(2,1)}) %all-gather.2.cloned.1.call-update) | async-done | bytes 8388624 | tf_op jit(solution)/shard_map/all_gather | solution.py:47
  89.3 6.3 %fusion.23 = bf16[4096,1,192]{0,2,1:T(8,128)(2,1)S(1)} fusion(bf16[4096,1024]{1,0:T(8,128)(2,1)} %all-gather.2.cloned.1.call-done, bf16[1024,1,64]{0,2,1:T(8,128)(2,1)S(1)} %slice-done, bf16[1024,1,128]{0,2,1:T(8,128)(2,1)S(1)} %slice-done.1), kind=kOutput, calls=%fused_computation.33 | convolution fusion | flops 1612185600 | bytes 10354688 | tf_op jit(solution)/shard_map/dot_general | solution.py:46
  99.4 15.0 %gather_fusion.1 = bf16[4096,128]{1,0:T(8,128)(2,1)} fusion(bf16[4096,128]{1,0:T(8,128)(2,1)S(1)} %copy.17, s32[4096]{0:T(1024)S(1)} %broadcast_clamp_fusion), kind=kCustom, calls=%fused_computation.3 | custom fusion | bytes 2113536 | tf_op jit(solution)/shard_map/jit(_take)/gather | solution.py:55
  114.4 3.4 broadcast_select_fusion.3
  118.3 25.5 %collective-permute-done = bf16[4096,128]{1,0:T(8,128)(2,1)S(1)} collective-permute-done((bf16[4096,128]{1,0:T(8,128)(2,1)S(1)}, bf16[4096,128]{1,0:T(8,128)(2,1)S(1)}, u32[]{:S(2)}, u32[]{:S(2)}) %collective-permute-start) | collective-permute-done | bytes 1048608 | tf_op jit(solution)/shard_map/ppermute | solution.py:16
  144.8 14.2 %collective-permute-done.1 = bf16[4096,128]{1,0:T(8,128)(2,1)S(1)} collective-permute-done((bf16[4096,128]{1,0:T(8,128)(2,1)S(1)}, bf16[4096,128]{1,0:T(8,128)(2,1)S(1)}, u32[]{:S(2)}, u32[]{:S(2)}) %collective-permute-start.1) | collective-permute-done | bytes 1048608 | tf_op jit(solution)/shard_map/ppermute | solution.py:16
  160.0 14.2 %collective-permute-done.2 = bf16[4096,128]{1,0:T(8,128)(2,1)S(1)} collective-permute-done((bf16[4096,128]{1,0:T(8,128)(2,1)S(1)}, bf16[4096,128]{1,0:T(8,128)(2,1)S(1)}, u32[]{:S(2)}, u32[]{:S(2)}) %collective-permute-start.2) | collective-permute-done | bytes 1048608 | tf_op jit(solution)/shard_map/ppermute | solution.py:16
  174.7 15.7 %scatter_custom_fusion = s32[4096]{0:T(1024)S(1)} fusion(s32[4096]{0:T(1024)S(1)} %bitcast.103, s32[4096]{0:T(1024)S(1)} %iota.3, s32[]{:T(128)} %copy.60), kind=kCustom, calls=%fused_computation.84 | custom fusion | bytes 16388 | tf_op jit(solution)/shard_map/scatter | solution.py:100
  190.5 3.7 collective-permute-start.4
  197.6 15.0 %gather_fusion.2 = bf16[4096,64]{1,0:T(8,128)(2,1)} fusion(bf16[4096,64]{1,0:T(8,128)(2,1)S(1)} %copy.18, s32[4096]{0:T(1024)S(1)} %get-tuple-element.53), kind=kCustom, calls=%fused_computation.clone | custom fusion | bytes 1064960 | tf_op jit(solution)/shard_map/jit(_take)/gather | solution.py:56
  212.6 3.4 broadcast_select_fusion.2
  221.4 2.3 copy-done.3
  223.7 92.5 %while.10 = (s32[]{:T(128)}, bf16[8,512,64]{1,2,0:T(8,128)(2,1)}, s32[8,4,8]{2,1,0:T(4,128)S(1)}, bf16[160,128,128]{2,1,0:T(8,128)(2,1)}, bf16[8,512,64]{1,2,0:T(8,128)(2,1)}, /*index=5*/s32[]{:T(128)}) while((s32[]{:T(128)}, bf16[8,512,64]{1,2,0:T(8,128)(2,1)}, s32[8,4,8]{2,1,0:T(4,128)S(1)}, bf16[160,128,128]{2,1,0:T(8,128)(2,1)}, ...), condition=%wide.region_5.7_spmd, body=%wide.region_2.6_spmd.sunk | while | flops 205557536 | bytes 12936373 | solution.py:94
  224.7 4.2 %gather_fusion = bf16[32,128,128]{2,1,0:T(8,128)(2,1)} fusion(bf16[160,128,128]{2,1,0:T(8,128)(2,1)} %get-tuple-element.105, s32[1024]{0:T(1024)S(1)} %pad_clamp_fusion.2), kind=kCustom, calls=%fused_computation.1.clone.1 | custom fusion | bytes 2097280 | tf_op jit(solution)/shard_map/while/body/eval_jaxpr/jit(_take)/gather | solution.py:73
  231.5 2.0 fusion.86
  236.3 4.2 %gather_fusion = bf16[32,128,128]{2,1,0:T(8,128)(2,1)} fusion(bf16[160,128,128]{2,1,0:T(8,128)(2,1)} %get-tuple-element.105, s32[1024]{0:T(1024)S(1)} %pad_clamp_fusion.2), kind=kCustom, calls=%fused_computation.1.clone.1 | custom fusion | bytes 2097280 | tf_op jit(solution)/shard_map/while/body/eval_jaxpr/jit(_take)/gather | solution.py:73
  243.1 2.0 fusion.86
  247.9 4.2 %gather_fusion = bf16[32,128,128]{2,1,0:T(8,128)(2,1)} fusion(bf16[160,128,128]{2,1,0:T(8,128)(2,1)} %get-tuple-element.105, s32[1024]{0:T(1024)S(1)} %pad_clamp_fusion.2), kind=kCustom, calls=%fused_computation.1.clone.1 | custom fusion | bytes 2097280 | tf_op jit(solution)/shard_map/while/body/eval_jaxpr/jit(_take)/gather | solution.py:73
  254.6 2.0 fusion.86
  259.4 4.2 %gather_fusion = bf16[32,128,128]{2,1,0:T(8,128)(2,1)} fusion(bf16[160,128,128]{2,1,0:T(8,128)(2,1)} %get-tuple-element.105, s32[1024]{0:T(1024)S(1)} %pad_clamp_fusion.2), kind=kCustom, calls=%fused_computation.1.clone.1 | custom fusion | bytes 2097280 | tf_op jit(solution)/shard_map/while/body/eval_jaxpr/jit(_take)/gather | solution.py:73
  266.2 2.0 fusion.86
  271.0 4.2 %gather_fusion = bf16[32,128,128]{2,1,0:T(8,128)(2,1)} fusion(bf16[160,128,128]{2,1,0:T(8,128)(2,1)} %get-tuple-element.105, s32[1024]{0:T(1024)S(1)} %pad_clamp_fusion.2), kind=kCustom, calls=%fused_computation.1.clone.1 | custom fusion | bytes 2097280 | tf_op jit(solution)/shard_map/while/body/eval_jaxpr/jit(_take)/gather | solution.py:73
  282.5 4.2 %gather_fusion = bf16[32,128,128]{2,1,0:T(8,128)(2,1)} fusion(bf16[160,128,128]{2,1,0:T(8,128)(2,1)} %get-tuple-element.105, s32[1024]{0:T(1024)S(1)} %pad_clamp_fusion.2), kind=kCustom, calls=%fused_computation.1.clone.1 | custom fusion | bytes 2097280 | tf_op jit(solution)/shard_map/while/body/eval_jaxpr/jit(_take)/gather | solution.py:73
  294.1 4.2 %gather_fusion = bf16[32,128,128]{2,1,0:T(8,128)(2,1)} fusion(bf16[160,128,128]{2,1,0:T(8,128)(2,1)} %get-tuple-element.105, s32[1024]{0:T(1024)S(1)} %pad_clamp_fusion.2), kind=kCustom, calls=%fused_computation.1.clone.1 | custom fusion | bytes 2097280 | tf_op jit(solution)/shard_map/while/body/eval_jaxpr/jit(_take)/gather | solution.py:73
  300.9 2.0 fusion.86
  305.7 4.2 %gather_fusion = bf16[32,128,128]{2,1,0:T(8,128)(2,1)} fusion(bf16[160,128,128]{2,1,0:T(8,128)(2,1)} %get-tuple-element.105, s32[1024]{0:T(1024)S(1)} %pad_clamp_fusion.2), kind=kCustom, calls=%fused_computation.1.clone.1 | custom fusion | bytes 2097280 | tf_op jit(solution)/shard_map/while/body/eval_jaxpr/jit(_take)/gather | solution.py:73
  312.4 2.0 fusion.86
  317.7 15.0 %gather_fusion.3 = bf16[4096,64]{1,0:T(8,128)(2,1)} fusion(bf16[4096,64]{1,0:T(8,128)(2,1)S(1)} %bitcast.94, s32[4096]{0:T(1024)S(1)} %get-tuple-element.54), kind=kCustom, calls=%fused_computation.2.clone | custom fusion | bytes 1064960 | tf_op jit(solution)/shard_map/jit(_take)/gather | solution.py:102
  332.7 4.3 %broadcast_select_fusion.1 = bf16[4096,64]{1,0:T(8,128)(2,1)} fusion(bf16[4096,64]{1,0:T(8,128)(2,1)} %gather_fusion.3, pred[4096]{0:T(1024)(128)(4,1)S(1)} %compare_and_fusion.1), kind=kLoop, calls=%fused_computation.65 | loop fusion | flops 262144 | bytes 1052672 | tf_op jit(solution)/shard_map/jit(_take)/select_n | solution.py:102
  338.5 16.7 %all_to_all.19 = bf16[16,256,64]{1,2,0:T(8,128)(2,1)S(1)} all-to-all(bf16[16,256,64]{1,2,0:T(8,128)(2,1)S(1)} %copy.21), channel_id=1, replica_groups=mesh['node'=16,'head'=16] {'head'}, dimensions={0} | all-to-all | bytes 1048576 | tf_op jit(solution)/shard_map/all_to_all | solution.py:103
  357.3 7.5 %fusion.32 = bf16[256,1024]{1,0:T(8,128)(2,1)} fusion(f32[256,1024]{1,0:T(8,128)} %copy-done.4, bf16[2048,1024]{1,0:T(8,128)(2,1)} %param.19, bf16[1024,2048]{1,0:T(8,128)(2,1)} %param.18, f32[1024]{0:T(1024)S(1)} %copy-done.14, f32[256]{0:T(256)S(1)} %add_rsqrt_fusion, f32[256]{0:T(256)S(1)} %broadcast_multiply_fusion), kind=kOutput, calls=%fused_computation.47 | convolution fusion | flops 2153775104 | bytes 9967616 | tf_op jit(solution)/shard_map/dot_general | solution.py:111
  (198 shorter events, 70.4 us)
Async XLA Ops:
  6.5 348.7 %copy-start = (bf16[1024,1024]{1,0:T(8,128)(2,1)S(1)}, bf16[1024,1024]{1,0:T(8,128)(2,1)}, u32[]{:S(2)}) copy-start(bf16[1024,1024]{1,0:T(8,128)(2,1)} %param.16) | copy-start | bytes 6291460
  6.5 82.7 %slice-start = ((bf16[1024,1,192]{0,2,1:T(8,128)(2,1)}), bf16[1024,1,64]{0,2,1:T(8,128)(2,1)S(1)}, s32[]{:S(2)}) async-start(bf16[1024,1,192]{0,2,1:T(8,128)(2,1)} %param.15), calls=%async_computation.2 | async-start | bytes 262144 | tf_op jit(solution)/shard_map/slice | solution.py:44
  6.5 82.7 %slice-start.1 = ((bf16[1024,1,192]{0,2,1:T(8,128)(2,1)}), bf16[1024,1,128]{0,2,1:T(8,128)(2,1)S(1)}, s32[]{:S(2)}) async-start(bf16[1024,1,192]{0,2,1:T(8,128)(2,1)} %param.15), calls=%async_computation.3 | async-start | bytes 524288 | tf_op jit(solution)/shard_map/slice | solution.py:44
  6.5 4.9 %copy-start.12 = (s32[1,4096]{1,0:T(1,128)S(1)}, s32[1,4096]{1,0:T(1,128)}, u32[]{:S(2)}) copy-start(s32[1,4096]{1,0:T(1,128)} %param.21) | copy-start | bytes 49156
  6.5 82.7 %all-gather.2.cloned.1.call-start = ((), (), s32[]{:S(2)}) async-start(), calls=%async_computation.1 | async-start | bytes 8912896 | tf_op jit(solution)/shard_map/all_gather | solution.py:47
  95.6 1.1 copy-start.5
  114.4 60.2 %copy-start.13 = (s32[32,8]{0,1:T(8,128)S(1)}, s32[32,8]{0,1:T(8,128)}, u32[]{:S(2)}) copy-start(s32[32,8]{0,1:T(8,128)} %param.20) | copy-start | bytes 3076
  117.8 26.0 %collective-permute-start = (bf16[4096,128]{1,0:T(8,128)(2,1)S(1)}, bf16[4096,128]{1,0:T(8,128)(2,1)S(1)}, u32[]{:S(2)}, u32[]{:S(2)}) collective-permute-start(bf16[4096,128]{1,0:T(8,128)(2,1)S(1)} %broadcast_select_fusion.3), channel_id=1, source_target_pairs={{0,224},{16,240},{32,0},{48,16},{64,32},{80,48},{96,64},{112,80},{... | collective-permute-start | bytes 3145736 | tf_op jit(solution)/shard_map/ppermute | solution.py:16
  143.8 1.0 copy-start.6
  144.8 14.2 %collective-permute-start.1 = (bf16[4096,128]{1,0:T(8,128)(2,1)S(1)}, bf16[4096,128]{1,0:T(8,128)(2,1)S(1)}, u32[]{:S(2)}, u32[]{:S(2)}) collective-permute-start(bf16[4096,128]{1,0:T(8,128)(2,1)S(1)} %collective-permute-done), channel_id=1, source_target_pairs={{0,16},{16,32},{32,48},{48,64},{64,80},{80,96},{96,112},{112,128},... | collective-permute-start | bytes 3145736 | tf_op jit(solution)/shard_map/ppermute | solution.py:16
  159.0 1.0 copy-start.8
  160.0 14.2 %collective-permute-start.2 = (bf16[4096,128]{1,0:T(8,128)(2,1)S(1)}, bf16[4096,128]{1,0:T(8,128)(2,1)S(1)}, u32[]{:S(2)}, u32[]{:S(2)}) collective-permute-start(bf16[4096,128]{1,0:T(8,128)(2,1)S(1)} %collective-permute-done.1), channel_id=1, source_target_pairs={{0,16},{16,32},{32,48},{48,64},{64,80},{80,96},{96,112},{112,128},... | collective-permute-start | bytes 3145736 | tf_op jit(solution)/shard_map/ppermute | solution.py:16
  174.2 20.0 %copy-start.10 = (bf16[4096,128]{1,0:T(8,128)(2,1)}, bf16[4096,128]{1,0:T(8,128)(2,1)S(1)}, u32[]{:S(2)}) copy-start(bf16[4096,128]{1,0:T(8,128)(2,1)S(1)} %collective-permute-done.2) | copy-start | bytes 3145732
  174.2 16.3 %collective-permute-start.3 = (bf16[4096,128]{1,0:T(8,128)(2,1)S(1)}, bf16[4096,128]{1,0:T(8,128)(2,1)}, u32[]{:S(2)}, u32[]{:S(2)}) collective-permute-start(bf16[4096,128]{1,0:T(8,128)(2,1)S(1)} %collective-permute-done.2), channel_id=1, source_target_pairs={{0,16},{16,32},{32,48},{48,64},{64,80},{80,96},{96,112},{112,128},... | collective-permute-start | bytes 3145736 | tf_op jit(solution)/shard_map/ppermute | solution.py:16
  190.5 26.6 %collective-permute-start.4 = (bf16[4096,128]{1,0:T(8,128)(2,1)}, bf16[4096,128]{1,0:T(8,128)(2,1)}, u32[]{:S(2)}, u32[]{:S(2)}) collective-permute-start(bf16[4096,128]{1,0:T(8,128)(2,1)} %collective-permute-done.3), channel_id=1, source_target_pairs={{0,16},{16,32},{32,48},{48,64},{64,80},{80,96},{96,112},{112,128},... | collective-permute-start | bytes 3145736 | tf_op jit(solution)/shard_map/ppermute | solution.py:16
  217.1 2.9 copy-start.11
  218.5 1.6 copy-start.9
  220.0 1.3 copy-start.7
  221.4 2.3 copy-start.3
  231.5 2.0 copy-start.1
  243.1 2.0 copy-start.1
  254.6 2.0 copy-start.1
  266.2 2.0 copy-start.1
  277.8 2.0 copy-start.1
  289.3 2.0 copy-start.1
  300.9 2.0 copy-start.1
  312.4 2.0 copy-start.1
  332.7 22.6 %copy-start.2 = (bf16[256,1024]{1,0:T(8,128)(2,1)S(1)}, bf16[256,1024]{1,0:T(8,128)(2,1)}, u32[]{:S(2)}) copy-start(bf16[256,1024]{1,0:T(8,128)(2,1)} %param.13) | copy-start | bytes 1572868
  355.2 2.1 copy-start.14
  356.1 1.0 copy-start.4
Sparse Core Ops, SparseCore 0:
  11.6 77.6 all-gather.1
where the time goes:
time: 373 us; the launch traced here: 372 us
  local copies, waits for them, and re-layouts  141 us (38%)
  waiting for transfers between devices  132 us (35%)
  matrix products  38.1 us (10%)
  other arithmetic  25.3 us (7%)
  blocking collectives  16.7 us (4%)
  between operations  13.6 us (4%)
  starting transfers between devices  4.69 us (1%)
    all_gather x1, waiting for transfers between devices, shards(): lax.all_gather(normed, 'head', axis=0, tiled=True)  77.8 us
    ppermute x5, waiting for transfers between devices, passed_along(): return lax.ppermute(x, axis, [(i, (i + by) % size) for i in range(size)])  53.9 us
    gather x16, local copies, waits for them, and re-layouts, attend(): picked = jnp.take(window_tiles, columns.reshape(tile_group * NNZ), axis=0)  45.3 us
    all_to_all x1, blocking collectives, shards(): lax.all_to_all(restored, 'head', split_axis=0, concat_axis=1, tiled=True)  16.7 us
    sub x8, matrix products, attend(): expd = jnp.exp(scores - row_max)  15.7 us
    scatter x1, local copies, waits for them, and re-layouts, shards(): inverse_order = jnp.zeros((rows_part,), jnp.int32).at[partition_permutati...  15.7 us
    gather x1, local copies, waits for them, and re-layouts, shards(): keyval = jnp.take(keyval_rows, partition_permutation, axis=0)  15 us
    gather x1, local copies, waits for them, and re-layouts, shards(): restored = jnp.take(attended, inverse_order, axis=0)  15 us
  transfers between devices with their start and end apart: 6, of which 4 were waited for; matrix products, arithmetic and copies ran while one was open for 10% of the time, Pallas kernels for 0%

commit v1 on v0

--- a/solution.py
+++ b/solution.py
@@ -9,6 +9,27 @@
 TILE = 128
 NNZ = 8
 REACH = 2
+
+
+def collect(x, axis, dim):
+    size, here, extent = (lax.axis_size(axis), lax.axis_index(axis), x.shape[dim])
+    right = [(i, (i + 1) % size) for i in range(size)]
+    behind = [(i, (i - 1) % size) for i in range(size)]
+    filled = jnp.zeros((*x.shape[:dim], size * extent, *x.shape[dim + 1 :]), x.dtype)
+    filled = lax.dynamic_update_slice_in_dim(filled, x, here * extent, axis=dim)
+    from_left = from_right = x
+    halfway = size // 2
+    for step in range(1, halfway + 1):
+        from_left = lax.ppermute(from_left, axis, right)
+        filled = lax.dynamic_update_slice_in_dim(
+            filled, from_left, (here - step) % size * extent, axis=dim
+        )
+        if step < size - halfway:
+            from_right = lax.ppermute(from_right, axis, behind)
+            filled = lax.dynamic_update_slice_in_dim(
+                filled, from_right, (here + step) % size * extent, axis=dim
+            )
+    return filled
 
 
 def passed_along(x, axis, by):
@@ -44,9 +65,7 @@
     reordered_weight = jnp.concatenate([qkv_weight[:, :, HD:], qkv_weight[:, :, :HD]], -1)
     local_weight = reordered_weight.reshape(D, local_heads * 3 * HD)
     projected = jnp.dot(
-        lax.all_gather(normed, "head", axis=0, tiled=True),
-        local_weight,
-        preferred_element_type=jnp.float32,
+        collect(normed, "head", 0), local_weight, preferred_element_type=jnp.float32
     ).astype(jnp.bfloat16)
     projected = projected.reshape(rows_part, local_heads, 3 * HD)
     partition_permutation = node_order[0]

time: 373 us -> 401 us (1.075)
  starting transfers between devices: 4.69 us -> 42.1 us
  waiting for transfers between devices: 132 us -> 106 us
  local copies, waits for them, and re-layouts: 141 us -> 164 us
  between operations: 13.6 us -> 0.66 us
  matrix products: 38.1 us -> 47.6 us
    all_gather x1 -> x0, waiting for transfers between devices: 77.8 us -> none  [shards(): lax.all_gather(normed, 'head', axis=0, tiled=True)]
    ppermute x0 -> x15, waiting for transfers between devices: none -> 59 us  [the longest x8 59 us: collect(): from_left = lax.ppermute(from_left, axis, right)]
    ppermute x0 -> x15, starting transfers between devices: none -> 37.6 us  [the longest x7 35.9 us: collect(): from_right = lax.ppermute(from_right, axis, behind)]
    dynamic_update_slice x0 -> x15, local copies, waits for them, and re-layouts: none -> 19.8 us  [the longest x7 9.97 us: collect(): lax.dynamic_update_slice_in_dim(filled, from_right, (here + step) % size...]
    dot_general x8, matrix products: 7.85 us -> 17.5 us  [attend(): jnp.einsum('ghqm,gmhd->gqhd', weight_arrays, value_rows, preferred_elemen...]
    ppermute x5, waiting for transfers between devices: 53.9 us -> 47.3 us  [passed_along(): return lax.ppermute(x, axis, [(i, (i + by) % size) for i in range(size)])]
    unnamed x32 -> x46, local copies, waits for them, and re-layouts: 10.4 us -> 13.1 us
  transfers between devices with their start and end apart: 6 -> 20, of which waited for: 4 -> 11; matrix products, arithmetic and copies ran while one was open for 10% -> 14% of each run, Pallas kernels for 0% -> 0%
where the time goes in v1:
time: 401 us; the launch traced here: 398 us
  local copies, waits for them, and re-layouts  164 us (41%)
  waiting for transfers between devices  106 us (26%)
  matrix products  47.6 us (12%)
  starting transfers between devices  42.1 us (10%)
  other arithmetic  22.3 us (6%)
  blocking collectives  15.5 us (4%)
    ppermute x8, waiting for transfers between devices, collect(): from_left = lax.ppermute(from_left, axis, right)  59 us
    ppermute x5, waiting for transfers between devices, passed_along(): return lax.ppermute(x, axis, [(i, (i + by) % size) for i in range(size)])  47.3 us
    gather x16, local copies, waits for them, and re-layouts, attend(): picked = jnp.take(window_tiles, columns.reshape(tile_group * NNZ), axis=0)  45 us
    ppermute x7, starting transfers between devices, collect(): from_right = lax.ppermute(from_right, axis, behind)  35.9 us
    dot_general x8, matrix products, attend(): jnp.einsum('ghqm,gmhd->gqhd', weight_arrays, value_rows, preferred_elemen...  17.5 us
    scatter x1, local copies, waits for them, and re-layouts, shards(): inverse_order = jnp.zeros((rows_part,), jnp.int32).at[partition_permutati...  15.7 us
    all_to_all x1, blocking collectives, shards(): lax.all_to_all(restored, 'head', split_axis=0, concat_axis=1, tiled=True)  15.5 us
    sub x8, matrix products, attend(): expd = jnp.exp(scores - row_max)  15.1 us
  transfers between devices with their start and end apart: 20, of which 11 were waited for; matrix products, arithmetic and copies ran while one was open for 14% of the time, Pallas kernels for 0%

profile of v1, /device:TPU:96, one launch (start us, length us, event | category | flops | bytes accessed | tf_op | source)
XLA Modules:
  0.0 398.4 jit_solution(15056035523091115217)
XLA Ops:
  9.0 3.8 collective-permute-start.1
  12.7 11.8 %collective-permute-done = bf16[256,1024]{1,0:T(8,128)(2,1)S(1)} collective-permute-done((bf16[256,1024]{1,0:T(8,128)(2,1)S(1)}, bf16[256,1024]{1,0:T(8,128)(2,1)S(1)}, u32[]{:S(2)}, u32[]{:S(2)}) %collective-permute-start) | collective-permute-done | bytes 524320 | tf_op jit(solution)/shard_map/ppermute | solution.py:23
  24.5 5.3 %collective-permute-start.3 = (bf16[256,1024]{1,0:T(8,128)(2,1)S(1)}, bf16[256,1024]{1,0:T(8,128)(2,1)S(1)}, u32[]{:S(2)}, u32[]{:S(2)}) collective-permute-start(bf16[256,1024]{1,0:T(8,128)(2,1)S(1)} %collective-permute-done.1), channel_id=1, source_target_pairs={{0,15},{1,0},{2,1},{3,2},{4,3},{5,4},{6,5},{7,6},{8,7},{9,8},{10,9... | collective-permute-start | bytes 1572872 | tf_op jit(solution)/shard_map/ppermute | solution.py:28
  29.9 10.9 %collective-permute-done.2 = bf16[256,1024]{1,0:T(8,128)(2,1)S(1)} collective-permute-done((bf16[256,1024]{1,0:T(8,128)(2,1)S(1)}, bf16[256,1024]{1,0:T(8,128)(2,1)S(1)}, u32[]{:S(2)}, u32[]{:S(2)}) %collective-permute-start.2) | collective-permute-done | bytes 524320 | tf_op jit(solution)/shard_map/ppermute | solution.py:23
  40.8 5.3 %collective-permute-start.5 = (bf16[256,1024]{1,0:T(8,128)(2,1)S(1)}, bf16[256,1024]{1,0:T(8,128)(2,1)S(1)}, u32[]{:S(2)}, u32[]{:S(2)}) collective-permute-start(bf16[256,1024]{1,0:T(8,128)(2,1)S(1)} %collective-permute-done.3), channel_id=1, source_target_pairs={{0,15},{1,0},{2,1},{3,2},{4,3},{5,4},{6,5},{7,6},{8,7},{9,8},{10,9... | collective-permute-start | bytes 1572872 | tf_op jit(solution)/shard_map/ppermute | solution.py:28
  46.2 10.1 %collective-permute-done.4 = bf16[256,1024]{1,0:T(8,128)(2,1)S(1)} collective-permute-done((bf16[256,1024]{1,0:T(8,128)(2,1)S(1)}, bf16[256,1024]{1,0:T(8,128)(2,1)S(1)}, u32[]{:S(2)}, u32[]{:S(2)}) %collective-permute-start.4) | collective-permute-done | bytes 524320 | tf_op jit(solution)/shard_map/ppermute | solution.py:23
  56.2 5.3 %collective-permute-start.7 = (bf16[256,1024]{1,0:T(8,128)(2,1)S(1)}, bf16[256,1024]{1,0:T(8,128)(2,1)}, u32[]{:S(2)}, u32[]{:S(2)}) collective-permute-start(bf16[256,1024]{1,0:T(8,128)(2,1)S(1)} %collective-permute-done.5), channel_id=1, source_target_pairs={{0,15},{1,0},{2,1},{3,2},{4,3},{5,4},{6,5},{7,6},{8,7},{9,8},{10,9... | collective-permute-start | bytes 1572872 | tf_op jit(solution)/shard_map/ppermute | solution.py:28
  61.6 9.2 %collective-permute-done.6 = bf16[256,1024]{1,0:T(8,128)(2,1)S(1)} collective-permute-done((bf16[256,1024]{1,0:T(8,128)(2,1)S(1)}, bf16[256,1024]{1,0:T(8,128)(2,1)S(1)}, u32[]{:S(2)}, u32[]{:S(2)}) %collective-permute-start.6) | collective-permute-done | bytes 524320 | tf_op jit(solution)/shard_map/ppermute | solution.py:23
  71.0 5.4 %collective-permute-start.9 = (bf16[256,1024]{1,0:T(8,128)(2,1)}, bf16[256,1024]{1,0:T(8,128)(2,1)}, u32[]{:S(2)}, u32[]{:S(2)}) collective-permute-start(bf16[256,1024]{1,0:T(8,128)(2,1)} %collective-permute-done.7), channel_id=1, source_target_pairs={{0,15},{1,0},{2,1},{3,2},{4,3},{5,4},{6,5},{7,6},{8,7},{9,8},{10,9... | collective-permute-start | bytes 1572872 | tf_op jit(solution)/shard_map/ppermute | solution.py:28
  76.4 8.3 %collective-permute-done.8 = bf16[256,1024]{1,0:T(8,128)(2,1)} collective-permute-done((bf16[256,1024]{1,0:T(8,128)(2,1)S(1)}, bf16[256,1024]{1,0:T(8,128)(2,1)}, u32[]{:S(2)}, u32[]{:S(2)}) %collective-permute-start.8) | collective-permute-done | bytes 524320 | tf_op jit(solution)/shard_map/ppermute | solution.py:23
  89.6 5.3 %collective-permute-start.11 = (bf16[256,1024]{1,0:T(8,128)(2,1)}, bf16[256,1024]{1,0:T(8,128)(2,1)S(1)}, u32[]{:S(2)}, u32[]{:S(2)}) collective-permute-start(bf16[256,1024]{1,0:T(8,128)(2,1)} %collective-permute-done.9), channel_id=1, source_target_pairs={{0,15},{1,0},{2,1},{3,2},{4,3},{5,4},{6,5},{7,6},{8,7},{9,8},{10,9... | collective-permute-start | bytes 1572872 | tf_op jit(solution)/shard_map/ppermute | solution.py:28
  102.2 5.5 %collective-permute-start.13 = (bf16[256,1024]{1,0:T(8,128)(2,1)S(1)}, bf16[256,1024]{1,0:T(8,128)(2,1)S(1)}, u32[]{:S(2)}, u32[]{:S(2)}) collective-permute-start(bf16[256,1024]{1,0:T(8,128)(2,1)S(1)} %collective-permute-done.11), channel_id=1, source_target_pairs={{0,15},{1,0},{2,1},{3,2},{4,3},{5,4},{6,5},{7,6},{8,7},{9,8},{10,9... | collective-permute-start | bytes 1572872 | tf_op jit(solution)/shard_map/ppermute | solution.py:28
  117.2 6.3 %collective-permute-done.14 = bf16[256,1024]{1,0:T(8,128)(2,1)S(1)} collective-permute-done((bf16[256,1024]{1,0:T(8,128)(2,1)S(1)}, bf16[256,1024]{1,0:T(8,128)(2,1)S(1)}, u32[]{:S(2)}, u32[]{:S(2)}) %collective-permute-start.14) | collective-permute-done | bytes 524320 | tf_op jit(solution)/shard_map/ppermute | solution.py:23
  124.3 6.3 %fusion.23 = bf16[4096,1,192]{0,2,1:T(8,128)(2,1)S(1)} fusion(bf16[4096,1024]{1,0:T(8,128)(2,1)} %constant_dynamic-update-slice_fusion.1, bf16[1024,1,64]{0,2,1:T(8,128)(2,1)S(1)} %slice-done.1, bf16[1024,1,128]{0,2,1:T(8,128)(2,1)S(1)} %slice-done), kind=kOutput, calls=%fused_computation.33 | convolution fusion | flops 1612185600 | bytes 10354688 | tf_op jit(solution)/shard_map/dot_general | solution.py:67
  134.4 14.9 %gather_fusion.1 = bf16[4096,128]{1,0:T(8,128)(2,1)} fusion(bf16[4096,128]{1,0:T(8,128)(2,1)S(1)} %copy.17, s32[4096]{0:T(1024)S(1)} %broadcast_clamp_fusion), kind=kCustom, calls=%fused_computation.3 | custom fusion | bytes 2113536 | tf_op jit(solution)/shard_map/jit(_take)/gather | solution.py:74
  152.9 18.9 %collective-permute-done.15 = bf16[4096,128]{1,0:T(8,128)(2,1)S(1)} collective-permute-done((bf16[4096,128]{1,0:T(8,128)(2,1)S(1)}, bf16[4096,128]{1,0:T(8,128)(2,1)S(1)}, u32[]{:S(2)}, u32[]{:S(2)}) %collective-permute-start.15) | collective-permute-done | bytes 1048608 | tf_op jit(solution)/shard_map/ppermute | solution.py:37
  172.8 14.2 %collective-permute-done.16 = bf16[4096,128]{1,0:T(8,128)(2,1)S(1)} collective-permute-done((bf16[4096,128]{1,0:T(8,128)(2,1)S(1)}, bf16[4096,128]{1,0:T(8,128)(2,1)S(1)}, u32[]{:S(2)}, u32[]{:S(2)}) %collective-permute-start.16) | collective-permute-done | bytes 1048608 | tf_op jit(solution)/shard_map/ppermute | solution.py:37
  188.0 14.2 %collective-permute-done.17 = bf16[4096,128]{1,0:T(8,128)(2,1)S(1)} collective-permute-done((bf16[4096,128]{1,0:T(8,128)(2,1)S(1)}, bf16[4096,128]{1,0:T(8,128)(2,1)S(1)}, u32[]{:S(2)}, u32[]{:S(2)}) %collective-permute-start.17) | collective-permute-done | bytes 1048608 | tf_op jit(solution)/shard_map/ppermute | solution.py:37
  202.8 15.7 %scatter_custom_fusion = s32[4096]{0:T(1024)S(1)} fusion(s32[4096]{0:T(1024)S(1)} %bitcast.102, s32[4096]{0:T(1024)S(1)} %iota.3, s32[]{:T(128)} %copy.76), kind=kCustom, calls=%fused_computation.84 | custom fusion | bytes 16388 | tf_op jit(solution)/shard_map/scatter | solution.py:119
  225.8 14.9 %gather_fusion.2 = bf16[4096,64]{1,0:T(8,128)(2,1)} fusion(bf16[4096,64]{1,0:T(8,128)(2,1)S(1)} %copy.18, s32[4096]{0:T(1024)S(1)} %get-tuple-element.55), kind=kCustom, calls=%fused_computation.clone | custom fusion | bytes 1064960 | tf_op jit(solution)/shard_map/jit(_take)/gather | solution.py:75
  252.1 100.8 %while.10 = (s32[]{:T(128)}, bf16[8,512,64]{1,2,0:T(8,128)(2,1)}, s32[8,4,8]{2,1,0:T(4,128)S(1)}, bf16[160,128,128]{2,1,0:T(8,128)(2,1)}, bf16[8,512,64]{1,2,0:T(8,128)(2,1)}, /*index=5*/s32[]{:T(128)}) while((s32[]{:T(128)}, bf16[8,512,64]{1,2,0:T(8,128)(2,1)}, s32[8,4,8]{2,1,0:T(4,128)S(1)}, bf16[160,128,128]{2,1,0:T(8,128)(2,1)}, ...), condition=%wide.region_5.7_spmd, body=%wide.region_2.0_spmd.sunk | while | flops 205557536 | bytes 8742541 | solution.py:113
  252.2 4.1 %gather_fusion = bf16[32,128,128]{2,1,0:T(8,128)(2,1)} fusion(bf16[160,128,128]{2,1,0:T(8,128)(2,1)} %get-tuple-element.107, s32[1024]{0:T(1024)S(1)} %pad_clamp_fusion.2), kind=kCustom, calls=%fused_computation.1.clone.1 | custom fusion | bytes 2097280 | tf_op jit(solution)/shard_map/while/body/eval_jaxpr/jit(_take)/gather | solution.py:92
  264.8 4.1 %gather_fusion = bf16[32,128,128]{2,1,0:T(8,128)(2,1)} fusion(bf16[160,128,128]{2,1,0:T(8,128)(2,1)} %get-tuple-element.107, s32[1024]{0:T(1024)S(1)} %pad_clamp_fusion.2), kind=kCustom, calls=%fused_computation.1.clone.1 | custom fusion | bytes 2097280 | tf_op jit(solution)/shard_map/while/body/eval_jaxpr/jit(_take)/gather | solution.py:92
  277.4 4.1 %gather_fusion = bf16[32,128,128]{2,1,0:T(8,128)(2,1)} fusion(bf16[160,128,128]{2,1,0:T(8,128)(2,1)} %get-tuple-element.107, s32[1024]{0:T(1024)S(1)} %pad_clamp_fusion.2), kind=kCustom, calls=%fused_computation.1.clone.1 | custom fusion | bytes 2097280 | tf_op jit(solution)/shard_map/while/body/eval_jaxpr/jit(_take)/gather | solution.py:92
  289.9 4.1 %gather_fusion = bf16[32,128,128]{2,1,0:T(8,128)(2,1)} fusion(bf16[160,128,128]{2,1,0:T(8,128)(2,1)} %get-tuple-element.107, s32[1024]{0:T(1024)S(1)} %pad_clamp_fusion.2), kind=kCustom, calls=%fused_computation.1.clone.1 | custom fusion | bytes 2097280 | tf_op jit(solution)/shard_map/while/body/eval_jaxpr/jit(_take)/gather | solution.py:92
  302.5 4.1 %gather_fusion = bf16[32,128,128]{2,1,0:T(8,128)(2,1)} fusion(bf16[160,128,128]{2,1,0:T(8,128)(2,1)} %get-tuple-element.107, s32[1024]{0:T(1024)S(1)} %pad_clamp_fusion.2), kind=kCustom, calls=%fused_computation.1.clone.1 | custom fusion | bytes 2097280 | tf_op jit(solution)/shard_map/while/body/eval_jaxpr/jit(_take)/gather | solution.py:92
  315.1 4.1 %gather_fusion = bf16[32,128,128]{2,1,0:T(8,128)(2,1)} fusion(bf16[160,128,128]{2,1,0:T(8,128)(2,1)} %get-tuple-element.107, s32[1024]{0:T(1024)S(1)} %pad_clamp_fusion.2), kind=kCustom, calls=%fused_computation.1.clone.1 | custom fusion | bytes 2097280 | tf_op jit(solution)/shard_map/while/body/eval_jaxpr/jit(_take)/gather | solution.py:92
  327.7 4.1 %gather_fusion = bf16[32,128,128]{2,1,0:T(8,128)(2,1)} fusion(bf16[160,128,128]{2,1,0:T(8,128)(2,1)} %get-tuple-element.107, s32[1024]{0:T(1024)S(1)} %pad_clamp_fusion.2), kind=kCustom, calls=%fused_computation.1.clone.1 | custom fusion | bytes 2097280 | tf_op jit(solution)/shard_map/while/body/eval_jaxpr/jit(_take)/gather | solution.py:92
  340.3 4.1 %gather_fusion = bf16[32,128,128]{2,1,0:T(8,128)(2,1)} fusion(bf16[160,128,128]{2,1,0:T(8,128)(2,1)} %get-tuple-element.107, s32[1024]{0:T(1024)S(1)} %pad_clamp_fusion.2), kind=kCustom, calls=%fused_computation.1.clone.1 | custom fusion | bytes 2097280 | tf_op jit(solution)/shard_map/while/body/eval_jaxpr/jit(_take)/gather | solution.py:92
  354.3 14.9 %gather_fusion.3 = bf16[4096,64]{1,0:T(8,128)(2,1)} fusion(bf16[4096,64]{1,0:T(8,128)(2,1)S(1)} %bitcast.93, s32[4096]{0:T(1024)S(1)} %get-tuple-element.56), kind=kCustom, calls=%fused_computation.2.clone | custom fusion | bytes 1064960 | tf_op jit(solution)/shard_map/jit(_take)/gather | solution.py:121
  373.8 15.5 %all_to_all.19 = bf16[16,256,64]{1,2,0:T(8,128)(2,1)S(1)} all-to-all(bf16[16,256,64]{1,2,0:T(8,128)(2,1)} %copy.21), channel_id=1, replica_groups=mesh['node'=16,'head'=16] {'head'}, dimensions={0} | all-to-all | bytes 1048576 | tf_op jit(solution)/shard_map/all_to_all | solution.py:122
  391.4 6.9 %fusion.32 = bf16[256,1024]{1,0:T(8,128)(2,1)} fusion(f32[256,1024]{1,0:T(8,128)S(1)} %get-tuple-element.54, bf16[2048,1024]{1,0:T(8,128)(2,1)} %param.19, bf16[1024,2048]{1,0:T(8,128)(2,1)} %param.18, f32[1024]{0:T(1024)S(1)} %copy-done.20, f32[256]{0:T(256)S(1)} %add_rsqrt_fusion, f32[256]{0:T(256)S(1)} %broadcast_multiply_fusion), kind=kOutput, calls=%fused_computation.47 | convolution fusion | flops 2153775104 | bytes 9967616 | tf_op jit(solution)/shard_map/dot_general | solution.py:130
  (239 shorter events, 135.3 us)
Async XLA Ops:
  0.0 389.3 %copy-start = (bf16[1024,1024]{1,0:T(8,128)(2,1)S(1)}, bf16[1024,1024]{1,0:T(8,128)(2,1)}, u32[]{:S(2)}) copy-start(bf16[1024,1024]{1,0:T(8,128)(2,1)} %param.16) | copy-start | bytes 6291460
  1.4 69.5 %copy-start.17 = (s32[1,4096]{1,0:T(1,128)S(1)}, s32[1,4096]{1,0:T(1,128)}, u32[]{:S(2)}) copy-start(s32[1,4096]{1,0:T(1,128)} %param.21) | copy-start | bytes 49156
  7.4 17.1 %collective-permute-start = (bf16[256,1024]{1,0:T(8,128)(2,1)S(1)}, bf16[256,1024]{1,0:T(8,128)(2,1)S(1)}, u32[]{:S(2)}, u32[]{:S(2)}) collective-permute-start(bf16[256,1024]{1,0:T(8,128)(2,1)S(1)} %get-tuple-element.52), channel_id=1, source_target_pairs={{0,1},{1,2},{2,3},{3,4},{4,5},{5,6},{6,7},{7,8},{8,9},{9,10},{10,1... | collective-permute-start | bytes 1572872 | tf_op jit(solution)/shard_map/ppermute | solution.py:23
  9.0 15.6 %collective-permute-start.1 = (bf16[256,1024]{1,0:T(8,128)(2,1)S(1)}, bf16[256,1024]{1,0:T(8,128)(2,1)S(1)}, u32[]{:S(2)}, u32[]{:S(2)}) collective-permute-start(bf16[256,1024]{1,0:T(8,128)(2,1)S(1)} %get-tuple-element.52), channel_id=1, source_target_pairs={{0,15},{1,0},{2,1},{3,2},{4,3},{5,4},{6,5},{7,6},{8,7},{9,8},{10,9... | collective-permute-start | bytes 1572872 | tf_op jit(solution)/shard_map/ppermute | solution.py:28
  24.5 16.3 %collective-permute-start.2 = (bf16[256,1024]{1,0:T(8,128)(2,1)S(1)}, bf16[256,1024]{1,0:T(8,128)(2,1)S(1)}, u32[]{:S(2)}, u32[]{:S(2)}) collective-permute-start(bf16[256,1024]{1,0:T(8,128)(2,1)S(1)} %collective-permute-done), channel_id=1, source_target_pairs={{0,1},{1,2},{2,3},{3,4},{4,5},{5,6},{6,7},{7,8},{8,9},{9,10},{10,1... | collective-permute-start | bytes 1572872 | tf_op jit(solution)/shard_map/ppermute | solution.py:23
  24.5 46.4 %copy-start.12 = (bf16[256,1024]{1,0:T(8,128)(2,1)}, bf16[256,1024]{1,0:T(8,128)(2,1)S(1)}, u32[]{:S(2)}) copy-start(bf16[256,1024]{1,0:T(8,128)(2,1)S(1)} %collective-permute-done.1) | copy-start | bytes 1572868
  24.5 16.3 %collective-permute-start.3 = (bf16[256,1024]{1,0:T(8,128)(2,1)S(1)}, bf16[256,1024]{1,0:T(8,128)(2,1)S(1)}, u32[]{:S(2)}, u32[]{:S(2)}) collective-permute-start(bf16[256,1024]{1,0:T(8,128)(2,1)S(1)} %collective-permute-done.1), channel_id=1, source_target_pairs={{0,15},{1,0},{2,1},{3,2},{4,3},{5,4},{6,5},{7,6},{8,7},{9,8},{10,9... | collective-permute-start | bytes 1572872 | tf_op jit(solution)/shard_map/ppermute | solution.py:28
  40.8 30.0 %copy-start.16 = (bf16[256,1024]{1,0:T(8,128)(2,1)}, bf16[256,1024]{1,0:T(8,128)(2,1)S(1)}, u32[]{:S(2)}) copy-start(bf16[256,1024]{1,0:T(8,128)(2,1)S(1)} %collective-permute-done.2) | copy-start | bytes 1572868
  40.8 15.4 %collective-permute-start.4 = (bf16[256,1024]{1,0:T(8,128)(2,1)S(1)}, bf16[256,1024]{1,0:T(8,128)(2,1)S(1)}, u32[]{:S(2)}, u32[]{:S(2)}) collective-permute-start(bf16[256,1024]{1,0:T(8,128)(2,1)S(1)} %collective-permute-done.2), channel_id=1, source_target_pairs={{0,1},{1,2},{2,3},{3,4},{4,5},{5,6},{6,7},{7,8},{8,9},{9,10},{10,1... | collective-permute-start | bytes 1572872 | tf_op jit(solution)/shard_map/ppermute | solution.py:23
  40.8 30.0 %copy-start.13 = (bf16[256,1024]{1,0:T(8,128)(2,1)}, bf16[256,1024]{1,0:T(8,128)(2,1)S(1)}, u32[]{:S(2)}) copy-start(bf16[256,1024]{1,0:T(8,128)(2,1)S(1)} %collective-permute-done.3) | copy-start | bytes 1572868
  40.8 15.4 %collective-permute-start.5 = (bf16[256,1024]{1,0:T(8,128)(2,1)S(1)}, bf16[256,1024]{1,0:T(8,128)(2,1)S(1)}, u32[]{:S(2)}, u32[]{:S(2)}) collective-permute-start(bf16[256,1024]{1,0:T(8,128)(2,1)S(1)} %collective-permute-done.3), channel_id=1, source_target_pairs={{0,15},{1,0},{2,1},{3,2},{4,3},{5,4},{6,5},{7,6},{8,7},{9,8},{10,9... | collective-permute-start | bytes 1572872 | tf_op jit(solution)/shard_map/ppermute | solution.py:28
  56.2 14.6 %collective-permute-start.6 = (bf16[256,1024]{1,0:T(8,128)(2,1)S(1)}, bf16[256,1024]{1,0:T(8,128)(2,1)S(1)}, u32[]{:S(2)}, u32[]{:S(2)}) collective-permute-start(bf16[256,1024]{1,0:T(8,128)(2,1)S(1)} %collective-permute-done.4), channel_id=1, source_target_pairs={{0,1},{1,2},{2,3},{3,4},{4,5},{5,6},{6,7},{7,8},{8,9},{9,10},{10,1... | collective-permute-start | bytes 1572872 | tf_op jit(solution)/shard_map/ppermute | solution.py:23
  56.2 14.6 %copy-start.10 = (bf16[256,1024]{1,0:T(8,128)(2,1)}, bf16[256,1024]{1,0:T(8,128)(2,1)S(1)}, u32[]{:S(2)}) copy-start(bf16[256,1024]{1,0:T(8,128)(2,1)S(1)} %collective-permute-done.5) | copy-start | bytes 1572868
  56.2 14.7 %collective-permute-start.7 = (bf16[256,1024]{1,0:T(8,128)(2,1)S(1)}, bf16[256,1024]{1,0:T(8,128)(2,1)}, u32[]{:S(2)}, u32[]{:S(2)}) collective-permute-start(bf16[256,1024]{1,0:T(8,128)(2,1)S(1)} %collective-permute-done.5), channel_id=1, source_target_pairs={{0,15},{1,0},{2,1},{3,2},{4,3},{5,4},{6,5},{7,6},{8,7},{9,8},{10,9... | collective-permute-start | bytes 1572872 | tf_op jit(solution)/shard_map/ppermute | solution.py:28
  70.8 13.9 %collective-permute-start.8 = (bf16[256,1024]{1,0:T(8,128)(2,1)S(1)}, bf16[256,1024]{1,0:T(8,128)(2,1)}, u32[]{:S(2)}, u32[]{:S(2)}) collective-permute-start(bf16[256,1024]{1,0:T(8,128)(2,1)S(1)} %collective-permute-done.6), channel_id=1, source_target_pairs={{0,1},{1,2},{2,3},{3,4},{4,5},{5,6},{6,7},{7,8},{8,9},{9,10},{10,1... | collective-permute-start | bytes 1572872 | tf_op jit(solution)/shard_map/ppermute | solution.py:23
  71.0 18.7 %collective-permute-start.9 = (bf16[256,1024]{1,0:T(8,128)(2,1)}, bf16[256,1024]{1,0:T(8,128)(2,1)}, u32[]{:S(2)}, u32[]{:S(2)}) collective-permute-start(bf16[256,1024]{1,0:T(8,128)(2,1)} %collective-permute-done.7), channel_id=1, source_target_pairs={{0,15},{1,0},{2,1},{3,2},{4,3},{5,4},{6,5},{7,6},{8,7},{9,8},{10,9... | collective-permute-start | bytes 1572872 | tf_op jit(solution)/shard_map/ppermute | solution.py:28
  84.7 13.2 %collective-permute-start.10 = (bf16[256,1024]{1,0:T(8,128)(2,1)}, bf16[256,1024]{1,0:T(8,128)(2,1)}, u32[]{:S(2)}, u32[]{:S(2)}) collective-permute-start(bf16[256,1024]{1,0:T(8,128)(2,1)} %collective-permute-done.8), channel_id=1, source_target_pairs={{0,1},{1,2},{2,3},{3,4},{4,5},{5,6},{6,7},{7,8},{8,9},{9,10},{10,1... | collective-permute-start | bytes 1572872 | tf_op jit(solution)/shard_map/ppermute | solution.py:23
  85.0 14.5 %copy-start.15 = (bf16[256,1024]{1,0:T(8,128)(2,1)S(1)}, bf16[256,1024]{1,0:T(8,128)(2,1)}, u32[]{:S(2)}) copy-start(bf16[256,1024]{1,0:T(8,128)(2,1)} %copy-done.14) | copy-start | bytes 1572868
  89.6 12.6 %collective-permute-start.11 = (bf16[256,1024]{1,0:T(8,128)(2,1)}, bf16[256,1024]{1,0:T(8,128)(2,1)S(1)}, u32[]{:S(2)}, u32[]{:S(2)}) collective-permute-start(bf16[256,1024]{1,0:T(8,128)(2,1)} %collective-permute-done.9), channel_id=1, source_target_pairs={{0,15},{1,0},{2,1},{3,2},{4,3},{5,4},{6,5},{7,6},{8,7},{9,8},{10,9... | collective-permute-start | bytes 1572872 | tf_op jit(solution)/shard_map/ppermute | solution.py:28
  97.8 13.1 %collective-permute-start.12 = (bf16[256,1024]{1,0:T(8,128)(2,1)}, bf16[256,1024]{1,0:T(8,128)(2,1)S(1)}, u32[]{:S(2)}, u32[]{:S(2)}) collective-permute-start(bf16[256,1024]{1,0:T(8,128)(2,1)} %collective-permute-done.10), channel_id=1, source_target_pairs={{0,1},{1,2},{2,3},{3,4},{4,5},{5,6},{6,7},{7,8},{8,9},{9,10},{10,1... | collective-permute-start | bytes 1572872 | tf_op jit(solution)/shard_map/ppermute | solution.py:23
  98.7 25.6 %slice-start = ((bf16[1024,1,192]{0,2,1:T(8,128)(2,1)}), bf16[1024,1,128]{0,2,1:T(8,128)(2,1)S(1)}, s32[]{:S(2)}) async-start(bf16[1024,1,192]{0,2,1:T(8,128)(2,1)} %param.15), calls=%async_computation.1 | async-start | bytes 524288 | tf_op jit(solution)/shard_map/slice | solution.py:65
  98.7 25.6 %slice-start.1 = ((bf16[1024,1,192]{0,2,1:T(8,128)(2,1)}), bf16[1024,1,64]{0,2,1:T(8,128)(2,1)S(1)}, s32[]{:S(2)}) async-start(bf16[1024,1,192]{0,2,1:T(8,128)(2,1)} %param.15), calls=%async_computation.2 | async-start | bytes 262144 | tf_op jit(solution)/shard_map/slice | solution.py:65
  102.2 14.1 %collective-permute-start.13 = (bf16[256,1024]{1,0:T(8,128)(2,1)S(1)}, bf16[256,1024]{1,0:T(8,128)(2,1)S(1)}, u32[]{:S(2)}, u32[]{:S(2)}) collective-permute-start(bf16[256,1024]{1,0:T(8,128)(2,1)S(1)} %collective-permute-done.11), channel_id=1, source_target_pairs={{0,15},{1,0},{2,1},{3,2},{4,3},{5,4},{6,5},{7,6},{8,7},{9,8},{10,9... | collective-permute-start | bytes 1572872 | tf_op jit(solution)/shard_map/ppermute | solution.py:28
  110.9 12.5 %collective-permute-start.14 = (bf16[256,1024]{1,0:T(8,128)(2,1)S(1)}, bf16[256,1024]{1,0:T(8,128)(2,1)S(1)}, u32[]{:S(2)}, u32[]{:S(2)}) collective-permute-start(bf16[256,1024]{1,0:T(8,128)(2,1)S(1)} %collective-permute-done.12), channel_id=1, source_target_pairs={{0,1},{1,2},{2,3},{3,4},{4,5},{5,6},{6,7},{7,8},{8,9},{9,10},{10,1... | collective-permute-start | bytes 1572872 | tf_op jit(solution)/shard_map/ppermute | solution.py:23
  134.4 84.1 %copy-start.19 = (s32[32,8]{0,1:T(8,128)S(1)}, s32[32,8]{0,1:T(8,128)}, u32[]{:S(2)}) copy-start(s32[32,8]{0,1:T(8,128)} %param.20) | copy-start | bytes 3076
  152.7 19.1 %collective-permute-start.15 = (bf16[4096,128]{1,0:T(8,128)(2,1)S(1)}, bf16[4096,128]{1,0:T(8,128)(2,1)S(1)}, u32[]{:S(2)}, u32[]{:S(2)}) collective-permute-start(bf16[4096,128]{1,0:T(8,128)(2,1)S(1)} %broadcast_select_fusion.3), channel_id=1, source_target_pairs={{0,224},{16,240},{32,0},{48,16},{64,32},{80,48},{96,64},{112,80},{... | collective-permute-start | bytes 3145736 | tf_op jit(solution)/shard_map/ppermute | solution.py:37
  172.8 14.2 %collective-permute-start.16 = (bf16[4096,128]{1,0:T(8,128)(2,1)S(1)}, bf16[4096,128]{1,0:T(8,128)(2,1)S(1)}, u32[]{:S(2)}, u32[]{:S(2)}) collective-permute-start(bf16[4096,128]{1,0:T(8,128)(2,1)S(1)} %collective-permute-done.15), channel_id=1, source_target_pairs={{0,16},{16,32},{32,48},{48,64},{64,80},{80,96},{96,112},{112,128},... | collective-permute-start | bytes 3145736 | tf_op jit(solution)/shard_map/ppermute | solution.py:37
  188.0 14.2 %collective-permute-start.17 = (bf16[4096,128]{1,0:T(8,128)(2,1)S(1)}, bf16[4096,128]{1,0:T(8,128)(2,1)S(1)}, u32[]{:S(2)}, u32[]{:S(2)}) collective-permute-start(bf16[4096,128]{1,0:T(8,128)(2,1)S(1)} %collective-permute-done.16), channel_id=1, source_target_pairs={{0,16},{16,32},{32,48},{48,64},{64,80},{80,96},{96,112},{112,128},... | collective-permute-start | bytes 3145736 | tf_op jit(solution)/shard_map/ppermute | solution.py:37
  202.2 20.2 %copy-start.9 = (bf16[4096,128]{1,0:T(8,128)(2,1)}, bf16[4096,128]{1,0:T(8,128)(2,1)S(1)}, u32[]{:S(2)}) copy-start(bf16[4096,128]{1,0:T(8,128)(2,1)S(1)} %collective-permute-done.17) | copy-start | bytes 3145732
  202.2 16.5 %collective-permute-start.18 = (bf16[4096,128]{1,0:T(8,128)(2,1)S(1)}, bf16[4096,128]{1,0:T(8,128)(2,1)}, u32[]{:S(2)}, u32[]{:S(2)}) collective-permute-start(bf16[4096,128]{1,0:T(8,128)(2,1)S(1)} %collective-permute-done.17), channel_id=1, source_target_pairs={{0,16},{16,32},{32,48},{48,64},{64,80},{80,96},{96,112},{112,128},... | collective-permute-start | bytes 3145736 | tf_op jit(solution)/shard_map/ppermute | solution.py:37
  218.7 26.5 %collective-permute-start.19 = (bf16[4096,128]{1,0:T(8,128)(2,1)}, bf16[4096,128]{1,0:T(8,128)(2,1)}, u32[]{:S(2)}, u32[]{:S(2)}) collective-permute-start(bf16[4096,128]{1,0:T(8,128)(2,1)} %collective-permute-done.18), channel_id=1, source_target_pairs={{0,16},{16,32},{32,48},{48,64},{64,80},{80,96},{96,112},{112,128},... | collective-permute-start | bytes 3145736 | tf_op jit(solution)/shard_map/ppermute | solution.py:37
  369.3 22.2 %copy-start.20 = (f32[1024]{0:T(1024)S(1)}, f32[1024]{0:T(1024)}, u32[]{:S(2)}) copy-start(f32[1024]{0:T(1024)} %param.17) | copy-start | bytes 12292
  (11 other events, 44.1 us)
